TPU v7x, 32 devices: a whole 2x2x4 slice. The times are simulated.
32 devices in a mesh: leaf: 16 (over z, y, x), sub: 2 (over core).
Axes of the slice: x: 2, y: 2, z: 4, core: 2. Of those that a mesh axis runs over, the one named last changes fastest.
Arguments:
- probes: float32 [64, 32768], P(None, ('leaf', 'sub')), may hold values from -600 to 600
- points: float32 [3, 32768], P(None, ('leaf', 'sub')), may hold values from -4 to 4
- leaf_order: int32 [32768], P(('leaf', 'sub')), may hold values from 0 to 1023, as said below
- near_list: int32 [64, 4], P(('leaf', 'sub')), may hold values from 0 to 63, as said below
- far_leaf_list: int32 [64, 2], P(('leaf', 'sub')), may hold values from 0 to 63, as said below
- far_chip_list: int32 [16, 8], P('leaf'), may hold values from -1 to 15, as said below
- leaf_basis: float32 [64, 512, 256], P(('leaf', 'sub')), may hold values from -0.25 to 0.25
- transfer: float32 [64, 256, 256], P(('leaf', 'sub')), may hold values from -0.1875 to 0.1875
- far_leaf_blocks: float32 [128, 256, 256], P(('leaf', 'sub')), may hold values from -0.25 to 0.25
- far_chip_blocks: float32 [128, 256, 256], P('leaf'), may hold values from -0.125 to 0.125
Outputs:
- result: float32 [64, 32768], P(None, ('leaf', 'sub'))
Inputs may be any that keep to these rules, and one draw needn't show every extreme that they name: `leaf_order`: each device's block of 1024 consecutive entries is a permutation of 0 to 1023. `near_list`: row l lists 4 distinct leaves, l among them, all held by the devices l // 2 - 1 to l // 2 + 1 of the joined axis leaf+sub, counted around the cycle. `far_leaf_list`: row l lists the 2 leaves of those same three devices that row l of near_list leaves out. `far_chip_list`: row k lists distinct chip clusters at cycle distance 2 to 5 from k, one to 8 of them, the used entries first and -1 in the rest; some row uses all 8.
All inputs are finite; a program needn't handle non-finite values.
Results may differ from a plain program's by a relative error of at most 0.0003.
Values sent between devices are 32-bit elements; how exact they have to be, the bound alone decides.
No kernel may reach another device: no remote copies, remote signals or barrier semaphores. Data moves between devices by JAX's collectives and lax.ppermute only.
A program may use at most 64 MiB of HBM per device.

v0:
```python
import jax
import jax.numpy as jnp
from jax import lax
from jax.sharding import PartitionSpec as P

CHIP_SPAN = 4
highest = lax.Precision.HIGHEST
inverse_width = 0.5 / (0.15 * 0.15)
epsilon = 1e-06


def from_behind(block, axis, distance):
    devices = range(lax.axis_size(axis))
    route = [((i - distance) % len(devices), i) for i in devices]
    return lax.ppermute(block, axis, route)


def kernel_tiles(source_points, target_points):
    spread = source_points[0] - target_points[0]
    distance = spread * spread
    for coord_axis in (1, 2):
        spread = source_points[coord_axis] - target_points[coord_axis]
        distance = distance + spread * spread
    return jnp.exp(-inverse_width * distance)


def leaf_window(values):
    pieces = []
    for offset in (1, 0, -1):
        if offset == 0:
            pieces.append(values)
        else:
            pieces.append(from_behind(values, ("leaf", "sub"), offset))
    first_device = lax.axis_index(("leaf", "sub")) - 1
    return (jnp.concatenate(pieces, 1), first_device)


def couple_chips(stacked, slot_place, used_count, far_chip_blocks):

    def add_slot(slot_index, running):
        source = stacked[slot_place[slot_index]]
        return running + jnp.dot(
            source,
            far_chip_blocks[slot_index],
            precision=highest,
            preferred_element_type=jnp.float32,
        )

    start_value = jnp.zeros((stacked.shape[1], stacked.shape[2]), jnp.float32)
    return lax.fori_loop(0, used_count, add_slot, start_value)


def chip_level(upward, far_chip_list, far_chip_blocks):
    chip_count = lax.axis_size("leaf")
    chip_index = lax.axis_index("leaf")
    slot_ids = far_chip_list[0]
    used_count = jnp.sum((slot_ids >= 0).astype(jnp.int32))
    offsets = jnp.mod(slot_ids - chip_index, chip_count)
    slot_place = jnp.where(
        offsets <= CHIP_SPAN + 1, offsets - 2, CHIP_SPAN + chip_count - offsets - 2
    )
    slot_place = jnp.clip(slot_place, 0, 2 * CHIP_SPAN - 1)
    shift_list = [-distance for distance in range(2, CHIP_SPAN + 2)] + [
        distance for distance in range(2, CHIP_SPAN + 2)
    ]
    halves = lax.psum_scatter(upward, "sub", scatter_dimension=0, tiled=True)
    pieces = [from_behind(halves, "leaf", offset) for offset in shift_list]
    coupled_half = couple_chips(jnp.stack(pieces), slot_place, used_count, far_chip_blocks)
    coupled = lax.all_gather(coupled_half, "sub", axis=0, tiled=True)
    return coupled


def apply_matrix(
    sorted_values,
    kernels,
    near_index,
    leaf_basis,
    transfer,
    far_leaf_list,
    far_leaf_blocks,
    far_chip_list,
    far_chip_blocks,
    leaf_total,
):
    columns = sorted_values.shape[0]
    leaf_count, leaf_size, rank_size = leaf_basis.shape
    value_window, window_start = leaf_window(sorted_values)
    window_tiles = value_window.reshape(columns, -1, leaf_size)
    source_values = jnp.take(window_tiles, near_index, axis=1)
    near_part = jnp.einsum("clnp,lnpq->clq", source_values, kernels, precision=highest)
    own_tiles = sorted_values.reshape(columns, leaf_count, leaf_size)
    coefficients = jnp.einsum("clp,lpr->lcr", own_tiles, leaf_basis, precision=highest)
    pieces = []
    for offset in (1, 0, -1):
        if offset == 0:
            pieces.append(coefficients)
        else:
            pieces.append(from_behind(coefficients, ("leaf", "sub"), offset))
    coeff_stack = jnp.concatenate(pieces, 0)
    device_index = lax.axis_index(("leaf", "sub"))
    far_index = jnp.mod(far_leaf_list - (device_index - 1) * leaf_count, leaf_total)
    far_sources = jnp.take(coeff_stack, far_index.reshape(-1), axis=0).reshape(
        leaf_count, -1, columns, rank_size
    )
    leaf_blocks = far_leaf_blocks.reshape(leaf_count, -1, rank_size, rank_size)
    local_far = jnp.einsum("ljcr,ljrs->lcs", far_sources, leaf_blocks, precision=highest)
    upward = jnp.einsum("lcr,lrs->cs", coefficients, transfer, precision=highest)
    chip_part = chip_level(upward, far_chip_list, far_chip_blocks)
    downward = local_far + jnp.einsum("cs,lrs->lcr", chip_part, transfer, precision=highest)
    far_part = jnp.einsum("lcr,lpr->clp", downward, leaf_basis, precision=highest)
    return (near_part + far_part).reshape(columns, leaf_count * leaf_size)


def on_device(
    probes,
    points,
    leaf_order,
    near_list,
    far_leaf_list,
    far_chip_list,
    leaf_basis,
    transfer,
    far_leaf_blocks,
    far_chip_blocks,
):
    leaf_count, leaf_size, rank_size = leaf_basis.shape
    leaf_total = leaf_count * lax.axis_size(("leaf", "sub"))
    point_total = probes.shape[1] * lax.axis_size(("leaf", "sub"))
    sorted_probes = probes[:, leaf_order]
    sorted_points = points[:, leaf_order]
    point_window, first_device = leaf_window(sorted_points)
    near_index = jnp.mod(near_list - first_device * leaf_count, leaf_total)
    point_tiles = point_window.reshape(3, -1, leaf_size)
    source_points = jnp.take(point_tiles, near_index, axis=1)
    target_points = sorted_points.reshape(3, leaf_count, leaf_size)
    kernels = kernel_tiles(source_points[..., :, None], target_points[:, :, None, None, :])
    first_pass = apply_matrix(
        sorted_probes,
        kernels,
        near_index,
        leaf_basis,
        transfer,
        far_leaf_list,
        far_leaf_blocks,
        far_chip_list,
        far_chip_blocks,
        leaf_total,
    )
    squares = lax.psum(jnp.sum(first_pass * first_pass, axis=1), ("leaf", "sub"))
    column_scale = lax.rsqrt(squares / point_total + epsilon)
    second = apply_matrix(
        first_pass * column_scale[:, None],
        kernels,
        near_index,
        leaf_basis,
        transfer,
        far_leaf_list,
        far_leaf_blocks,
        far_chip_list,
        far_chip_blocks,
        leaf_total,
    )
    return jnp.zeros_like(second).at[:, leaf_order].set(second)


def solution(mesh):
    return jax.shard_map(
        on_device,
        mesh=mesh,
        in_specs=(
            P(None, ("leaf", "sub")),
            P(None, ("leaf", "sub")),
            P(("leaf", "sub")),
            P(("leaf", "sub"), None),
            P(("leaf", "sub"), None),
            P("leaf", None),
            P(("leaf", "sub"), None, None),
            P(("leaf", "sub"), None, None),
            P(("leaf", "sub"), None, None),
            P("leaf", None, None),
        ),
        out_specs=P(None, ("leaf", "sub")),
        check_vma=False,
    )
```

profile of v0, /device:TPU:5, one launch (start us, length us, event | category | flops | bytes accessed | tf_op | source)
XLA Modules:
  0.0 316.3 jit_solution(15570008534534858504)
XLA Ops:
  9.1 4.0 %gather_fusion.2 = f32[1024,64]{1,0:T(8,128)} fusion(f32[64,1024]{0,1:T(8,128)S(1)} %copy.43, s32[1024]{0:T(1024)S(1)} %get-tuple-element.107), kind=kCustom, calls=%fused_computation.6 | custom fusion | bytes 528384 | tf_op jit(solution)/shard_map/gather | solution.py:129
  18.9 3.8 %gather_fusion = f32[1024,3]{1,0:T(8,128)S(1)} fusion(f32[3,1024]{0,1:T(8,128)} %copy.39, s32[1024]{0:T(1024)S(1)} %get-tuple-element.107), kind=kCustom, calls=%fused_computation.4 | custom fusion | bytes 28672 | tf_op jit(solution)/shard_map/gather | solution.py:130
  45.1 5.9 %collective-permute-start.6 = (f32[32,256]{1,0:T(8,128)}, f32[32,256]{1,0:T(8,128)S(1)}, u32[]{:S(2)}, u32[]{:S(2)}) collective-permute-start(f32[32,256]{1,0:T(8,128)} %reduce-scatter.3.cloned.1.call-done), channel_id=1, source_target_pairs={{4,0},{6,2},{8,4},{10,6},{12,8},{14,10},{16,12},{18,14},{20,16},{2... | collective-permute-start | bytes 98312 | tf_op jit(solution)/shard_map/ppermute | solution.py:15
  54.9 10.9 %collective-permute-start.7 = (f32[32,256]{1,0:T(8,128)}, f32[32,256]{1,0:T(8,128)S(1)}, u32[]{:S(2)}, u32[]{:S(2)}) collective-permute-start(f32[32,256]{1,0:T(8,128)} %reduce-scatter.3.cloned.1.call-done), channel_id=1, source_target_pairs={{6,0},{8,2},{10,4},{12,6},{14,8},{16,10},{18,12},{20,14},{22,16},{... | collective-permute-start | bytes 98312 | tf_op jit(solution)/shard_map/ppermute | solution.py:15
  67.3 3.2 %collective-permute-done.8 = f32[32,256]{1,0:T(8,128)S(1)} collective-permute-done((f32[32,256]{1,0:T(8,128)}, f32[32,256]{1,0:T(8,128)S(1)}, u32[]{:S(2)}, u32[]{:S(2)}) %collective-permute-start.8) | collective-permute-done | bytes 32800 | tf_op jit(solution)/shard_map/ppermute | solution.py:15
  70.6 5.1 %collective-permute-start.9 = (f32[32,256]{1,0:T(8,128)}, f32[32,256]{1,0:T(8,128)S(1)}, u32[]{:S(2)}, u32[]{:S(2)}) collective-permute-start(f32[32,256]{1,0:T(8,128)} %reduce-scatter.3.cloned.1.call-done), channel_id=1, source_target_pairs={{10,0},{12,2},{14,4},{16,6},{18,8},{20,10},{22,12},{24,14},{26,16}... | collective-permute-start | bytes 98312 | tf_op jit(solution)/shard_map/ppermute | solution.py:15
  80.3 2.5 collective-permute-start.11
  82.8 3.7 %collective-permute-done.11 = f32[32,256]{1,0:T(8,128)S(1)} collective-permute-done((f32[32,256]{1,0:T(8,128)}, f32[32,256]{1,0:T(8,128)S(1)}, u32[]{:S(2)}, u32[]{:S(2)}) %collective-permute-start.11) | collective-permute-done | bytes 32800 | tf_op jit(solution)/shard_map/ppermute | solution.py:15
  87.2 38.6 %while.20 = (s32[]{:T(128)}, f32[32,256]{1,0:T(8,128)S(1)}, s32[]{:T(128)}, s32[8]{0:T(128)}, f32[8,32,256]{2,1,0:T(8,128)}, /*index=5*/f32[8,256,256]{2,1,0:T(8,128)}, s32[]{:T(128)}, s32[]{:T(128)}, s32[]{:T(128)}) while((s32[]{:T(128)}, f32[32,256]{1,0:T(8,128)S(1)}, s32[]{:T(128)}, s32[8]{0:T(128)}, f32[8,32,256]{2,1,0:T(8,128)}, ...), condition=%wide.region_3.6_spmd, body=%wide.region_2.5_spmd.sunk | while | flops 25174024 | bytes 360637 | solution.py:50
  125.8 3.8 %all_gather.6 = f32[64,256]{1,0:T(8,128)S(1)} all-gather(f32[32,256]{1,0:T(8,128)S(1)} %get-tuple-element.73), channel_id=1, replica_groups=mesh['leaf'=16,'sub'=2] {'sub'}, dimensions={0}, use_global_device_ids=true | all-gather | bytes 98304 | tf_op jit(solution)/shard_map/all_gather | solution.py:69
  130.3 2.5 pad_maximum_fusion
  132.7 3.6 %gather_fusion.3 = f32[8,64,512]{1,2,0:T(8,128)} fusion(f32[64,6,512]{0,2,1:T(8,128)} %bitcast.168, s32[1024]{0:T(1024)} %pad_clamp_fusion.1), kind=kCustom, calls=%fused_computation.clone | custom fusion | bytes 2097184 | tf_op jit(solution)/shard_map/jit(_take)/gather | solution.py:89
  136.3 3.2 %copy.44 = f32[8,64,512]{2,1,0:T(8,128)} copy(f32[8,64,512]{1,2,0:T(8,128)} %gather_fusion.3) | data formatting | bytes 2097152 | tf_op jit(solution)/shard_map/jit(_take)/gather | solution.py:89
  139.5 9.7 %fusion.26 = f32[64,2,512]{2,0,1:T(8,128)S(1)} fusion(f32[2,512]{1,0:T(2,128)S(1)} %copy-done.13, f32[2,4,512]{2,1,0:T(4,128)S(1)} %copy-done.5, f32[2,512]{1,0:T(2,128)S(1)} %copy-done.11, f32[2,4,512]{2,1,0:T(4,128)S(1)} %copy-done.7, f32[2,512]{1,0:T(2,128)S(1)} %copy-done.9, f32[2,4,512]{2,1,0:T(4,128)S(1)} %bitcast.184, ...), kind=kOutput, calls=%fused_computation.38 | convolution fusion | flops 1629749248 | bytes 1372168 | tf_op jit(solution)/shard_map/clnp,lnpq->clq/dot_general | solution.py:90
  150.5 39.2 %psum.7 = f32[64]{0:T(128)S(1)} all-reduce(f32[64]{0:T(128)S(1)} %get-tuple-element.109), channel_id=1, replica_groups=mesh['leaf'=16,'sub'=2] {'leaf','sub'}, use_global_device_ids=true, to_apply=%region_5.8 | all-reduce | flops 64 | bytes 512 | tf_op jit(solution)/shard_map/psum | solution.py:149
  199.2 10.4 %reduce-scatter.5.cloned.1.call-done = f32[32,256]{1,0:T(8,128)} async-done(((f32[64,256]{1,0:T(8,128)}), f32[32,256]{1,0:T(8,128)}) %reduce-scatter.5.cloned.1.call-update) | async-done | bytes 32784 | tf_op jit(solution)/shard_map/reduce_scatter | solution.py:66
  214.0 5.3 %collective-permute-start.19 = (f32[32,256]{1,0:T(8,128)}, f32[32,256]{1,0:T(8,128)S(1)}, u32[]{:S(2)}, u32[]{:S(2)}) collective-permute-start(f32[32,256]{1,0:T(8,128)} %reduce-scatter.5.cloned.1.call-done), channel_id=1, source_target_pairs={{6,0},{8,2},{10,4},{12,6},{14,8},{16,10},{18,12},{20,14},{22,16},{... | collective-permute-start | bytes 98312 | tf_op jit(solution)/shard_map/ppermute | solution.py:15
  220.6 4.5 %collective-permute-start.20 = (f32[32,256]{1,0:T(8,128)}, f32[32,256]{1,0:T(8,128)S(1)}, u32[]{:S(2)}, u32[]{:S(2)}) collective-permute-start(f32[32,256]{1,0:T(8,128)} %reduce-scatter.5.cloned.1.call-done), channel_id=1, source_target_pairs={{8,0},{10,2},{12,4},{14,6},{16,8},{18,10},{20,12},{22,14},{24,16},... | collective-permute-start | bytes 98312 | tf_op jit(solution)/shard_map/ppermute | solution.py:15
  226.4 2.6 collective-permute-start.21
  235.9 4.2 %collective-permute-done.23 = f32[32,256]{1,0:T(8,128)S(1)} collective-permute-done((f32[32,256]{1,0:T(8,128)}, f32[32,256]{1,0:T(8,128)S(1)}, u32[]{:S(2)}, u32[]{:S(2)}) %collective-permute-start.23) | collective-permute-done | bytes 32800 | tf_op jit(solution)/shard_map/ppermute | solution.py:15
  240.2 42.2 %while.21 = (s32[]{:T(128)}, f32[32,256]{1,0:T(8,128)S(1)}, s32[]{:T(128)}, s32[8]{0:T(128)}, f32[8,32,256]{2,1,0:T(8,128)S(1)}, /*index=5*/f32[8,256,256]{2,1,0:T(8,128)}, s32[]{:T(128)}, s32[]{:T(128)}, s32[]{:T(128)}) while((s32[]{:T(128)}, f32[32,256]{1,0:T(8,128)S(1)}, s32[]{:T(128)}, s32[8]{0:T(128)}, f32[8,32,256]{2,1,0:T(8,128)S(1)}, ...), condition=%wide.region_8.11_spmd, body=%wide.region_7.10_spmd.sunk | while | flops 25174024 | bytes 360637 | solution.py:50
  282.4 8.1 %all_gather.7 = f32[64,256]{1,0:T(8,128)S(1)} all-gather(f32[32,256]{1,0:T(8,128)S(1)} %get-tuple-element.74), channel_id=1, replica_groups=mesh['leaf'=16,'sub'=2] {'sub'}, dimensions={0}, use_global_device_ids=true | all-gather | bytes 98304 | tf_op jit(solution)/shard_map/all_gather | solution.py:69
  294.2 9.7 %fusion.27 = f32[64,2,512]{2,0,1:T(8,128)S(1)} fusion(f32[2,512]{1,0:T(2,128)S(1)} %copy-done.14, f32[2,4,512]{2,1,0:T(4,128)S(1)} %copy-done.6, f32[2,512]{1,0:T(2,128)S(1)} %copy-done.12, f32[2,4,512]{2,1,0:T(4,128)S(1)} %copy-done.8, f32[2,512]{1,0:T(2,128)S(1)} %copy-done.10, f32[2,4,512]{2,1,0:T(4,128)S(1)} %bitcast.185, ...), kind=kOutput, calls=%fused_computation.39 | convolution fusion | flops 1629749248 | bytes 1372168 | tf_op jit(solution)/shard_map/clnp,lnpq->clq/dot_general | solution.py:90
  305.2 3.3 %scatter_custom_fusion = f32[64,1024]{0,1:T(8,128)S(1)} fusion(s32[1024]{0:T(1024)} %get-tuple-element.108, f32[1024,64]{1,0:T(8,128)S(1)} %copy.49, f32[]{:T(128)} %constant.109.clone.1), kind=kCustom, calls=%fused_computation.71 | custom fusion | bytes 262656 | tf_op jit(solution)/shard_map/scatter | solution.py:163
  (190 shorter events, 112.2 us)
Async XLA Ops:
  6.5 38.6 %reduce-scatter.3.cloned.1.call-start = ((), (), s32[]{:S(2)}) async-start(), calls=%async_computation.2 | async-start | bytes 98304 | tf_op jit(solution)/shard_map/reduce_scatter | solution.py:66
  15.2 28.4 %collective-permute-start.5 = (f32[2,64,256]{2,1,0:T(8,128)S(1)}, f32[2,64,256]{2,1,0:T(8,128)S(1)}, u32[]{:S(2)}, u32[]{:S(2)}) collective-permute-start(f32[2,64,256]{2,1,0:T(8,128)S(1)} %fusion.58), channel_id=1, source_target_pairs={{1,0},{2,1},{3,2},{4,3},{5,4},{6,5},{7,6},{8,7},{9,8},{10,9},{11,1... | collective-permute-start | bytes 393224 | tf_op jit(solution)/shard_map/ppermute | solution.py:15
  15.9 27.7 %collective-permute-start.4 = (f32[2,64,256]{2,1,0:T(8,128)S(1)}, f32[2,64,256]{2,1,0:T(8,128)S(1)}, u32[]{:S(2)}, u32[]{:S(2)}) collective-permute-start(f32[2,64,256]{2,1,0:T(8,128)S(1)} %fusion.58), channel_id=1, source_target_pairs={{31,0},{0,1},{1,2},{2,3},{3,4},{4,5},{5,6},{6,7},{7,8},{8,9},{9,10... | collective-permute-start | bytes 393224 | tf_op jit(solution)/shard_map/ppermute | solution.py:15
  22.7 13.9 %collective-permute-start.1 = (f32[3,1024]{0,1:T(8,128)S(1)}, f32[3,1024]{0,1:T(8,128)}, u32[]{:S(2)}, u32[]{:S(2)}) collective-permute-start(f32[3,1024]{0,1:T(8,128)S(1)} %bitcast.164), channel_id=1, source_target_pairs={{1,0},{2,1},{3,2},{4,3},{5,4},{6,5},{7,6},{8,7},{9,8},{10,9},{11,1... | collective-permute-start | bytes 36872 | tf_op jit(solution)/shard_map/ppermute | solution.py:15
  22.8 16.8 %collective-permute-start = (f32[3,1024]{0,1:T(8,128)S(1)}, f32[3,1024]{0,1:T(8,128)}, u32[]{:S(2)}, u32[]{:S(2)}) collective-permute-start(f32[3,1024]{0,1:T(8,128)S(1)} %bitcast.165), channel_id=1, source_target_pairs={{31,0},{0,1},{1,2},{2,3},{3,4},{4,5},{5,6},{6,7},{7,8},{8,9},{9,10... | collective-permute-start | bytes 36872 | tf_op jit(solution)/shard_map/ppermute | solution.py:15
  25.6 184.0 %reduce-scatter.5.cloned.1.call-start = ((), (), s32[]{:S(2)}) async-start(), calls=%async_computation.3 | async-start | bytes 98304 | tf_op jit(solution)/shard_map/reduce_scatter | solution.py:66
  25.6 104.6 %collective-permute-start.3 = (f32[64,1024]{0,1:T(8,128)}, f32[64,1024]{0,1:T(8,128)}, u32[]{:S(2)}, u32[]{:S(2)}) collective-permute-start(f32[64,1024]{0,1:T(8,128)} %bitcast.171), channel_id=1, source_target_pairs={{1,0},{2,1},{3,2},{4,3},{5,4},{6,5},{7,6},{8,7},{9,8},{10,9},{11,1... | collective-permute-start | bytes 786440 | tf_op jit(solution)/shard_map/ppermute | solution.py:15
  36.6 93.6 %collective-permute-start.2 = (f32[64,1024]{0,1:T(8,128)}, f32[64,1024]{0,1:T(8,128)}, u32[]{:S(2)}, u32[]{:S(2)}) collective-permute-start(f32[64,1024]{0,1:T(8,128)} %bitcast.172), channel_id=1, source_target_pairs={{31,0},{0,1},{1,2},{2,3},{3,4},{4,5},{5,6},{6,7},{7,8},{8,9},{9,10... | collective-permute-start | bytes 786440 | tf_op jit(solution)/shard_map/ppermute | solution.py:15
  45.1 9.7 %collective-permute-start.6 = (f32[32,256]{1,0:T(8,128)}, f32[32,256]{1,0:T(8,128)S(1)}, u32[]{:S(2)}, u32[]{:S(2)}) collective-permute-start(f32[32,256]{1,0:T(8,128)} %reduce-scatter.3.cloned.1.call-done), channel_id=1, source_target_pairs={{4,0},{6,2},{8,4},{10,6},{12,8},{14,10},{16,12},{18,14},{20,16},{2... | collective-permute-start | bytes 98312 | tf_op jit(solution)/shard_map/ppermute | solution.py:15
  51.8 34.6 %collective-permute-start.13 = (f32[32,256]{1,0:T(8,128)}, f32[32,256]{1,0:T(8,128)S(1)}, u32[]{:S(2)}, u32[]{:S(2)}) collective-permute-start(f32[32,256]{1,0:T(8,128)} %reduce-scatter.3.cloned.1.call-done), channel_id=1, source_target_pairs={{22,0},{24,2},{26,4},{28,6},{30,8},{0,10},{2,12},{4,14},{6,16},{8,... | collective-permute-start | bytes 98312 | tf_op jit(solution)/shard_map/ppermute | solution.py:15
  53.6 32.9 %collective-permute-start.12 = (f32[32,256]{1,0:T(8,128)}, f32[32,256]{1,0:T(8,128)S(1)}, u32[]{:S(2)}, u32[]{:S(2)}) collective-permute-start(f32[32,256]{1,0:T(8,128)} %reduce-scatter.3.cloned.1.call-done), channel_id=1, source_target_pairs={{24,0},{26,2},{28,4},{30,6},{0,8},{2,10},{4,12},{6,14},{8,16},{10,... | collective-permute-start | bytes 98312 | tf_op jit(solution)/shard_map/ppermute | solution.py:15
  54.9 12.3 %collective-permute-start.7 = (f32[32,256]{1,0:T(8,128)}, f32[32,256]{1,0:T(8,128)S(1)}, u32[]{:S(2)}, u32[]{:S(2)}) collective-permute-start(f32[32,256]{1,0:T(8,128)} %reduce-scatter.3.cloned.1.call-done), channel_id=1, source_target_pairs={{6,0},{8,2},{10,4},{12,6},{14,8},{16,10},{18,12},{20,14},{22,16},{... | collective-permute-start | bytes 98312 | tf_op jit(solution)/shard_map/ppermute | solution.py:15
  70.6 6.4 %collective-permute-start.9 = (f32[32,256]{1,0:T(8,128)}, f32[32,256]{1,0:T(8,128)S(1)}, u32[]{:S(2)}, u32[]{:S(2)}) collective-permute-start(f32[32,256]{1,0:T(8,128)} %reduce-scatter.3.cloned.1.call-done), channel_id=1, source_target_pairs={{10,0},{12,2},{14,4},{16,6},{18,8},{20,10},{22,12},{24,14},{26,16}... | collective-permute-start | bytes 98312 | tf_op jit(solution)/shard_map/ppermute | solution.py:15
  80.3 6.1 %collective-permute-start.11 = (f32[32,256]{1,0:T(8,128)}, f32[32,256]{1,0:T(8,128)S(1)}, u32[]{:S(2)}, u32[]{:S(2)}) collective-permute-start(f32[32,256]{1,0:T(8,128)} %reduce-scatter.3.cloned.1.call-done), channel_id=1, source_target_pairs={{26,0},{28,2},{30,4},{0,6},{2,8},{4,10},{6,12},{8,14},{10,16},{12,... | collective-permute-start | bytes 98312 | tf_op jit(solution)/shard_map/ppermute | solution.py:15
  190.5 6.3 %collective-permute-start.17 = (f32[2,64,256]{2,1,0:T(8,128)S(1)}, f32[2,64,256]{2,1,0:T(8,128)S(1)}, u32[]{:S(2)}, u32[]{:S(2)}) collective-permute-start(f32[2,64,256]{2,1,0:T(8,128)S(1)} %fusion.41), channel_id=1, source_target_pairs={{1,0},{2,1},{3,2},{4,3},{5,4},{6,5},{7,6},{8,7},{9,8},{10,9},{11,1... | collective-permute-start | bytes 393224 | tf_op jit(solution)/shard_map/ppermute | solution.py:15
  191.7 5.1 %collective-permute-start.16 = (f32[2,64,256]{2,1,0:T(8,128)S(1)}, f32[2,64,256]{2,1,0:T(8,128)}, u32[]{:S(2)}, u32[]{:S(2)}) collective-permute-start(f32[2,64,256]{2,1,0:T(8,128)S(1)} %fusion.41), channel_id=1, source_target_pairs={{31,0},{0,1},{1,2},{2,3},{3,4},{4,5},{5,6},{6,7},{7,8},{8,9},{9,10... | collective-permute-start | bytes 393224 | tf_op jit(solution)/shard_map/ppermute | solution.py:15
  194.0 97.1 %collective-permute-start.15 = (f32[64,1024]{1,0:T(8,128)}, f32[64,1024]{1,0:T(8,128)}, u32[]{:S(2)}, u32[]{:S(2)}) collective-permute-start(f32[64,1024]{1,0:T(8,128)} %broadcast_multiply_fusion), channel_id=1, source_target_pairs={{1,0},{2,1},{3,2},{4,3},{5,4},{6,5},{7,6},{8,7},{9,8},{10,9},{11,1... | collective-permute-start | bytes 786440 | tf_op jit(solution)/shard_map/ppermute | solution.py:15
  194.0 97.1 %collective-permute-start.14 = (f32[64,1024]{1,0:T(8,128)}, f32[64,1024]{1,0:T(8,128)}, u32[]{:S(2)}, u32[]{:S(2)}) collective-permute-start(f32[64,1024]{1,0:T(8,128)} %broadcast_multiply_fusion), channel_id=1, source_target_pairs={{31,0},{0,1},{1,2},{2,3},{3,4},{4,5},{5,6},{6,7},{7,8},{8,9},{9,10... | collective-permute-start | bytes 786440 | tf_op jit(solution)/shard_map/ppermute | solution.py:15
  209.6 4.4 %collective-permute-start.18 = (f32[32,256]{1,0:T(8,128)}, f32[32,256]{1,0:T(8,128)S(1)}, u32[]{:S(2)}, u32[]{:S(2)}) collective-permute-start(f32[32,256]{1,0:T(8,128)} %reduce-scatter.5.cloned.1.call-done), channel_id=1, source_target_pairs={{4,0},{6,2},{8,4},{10,6},{12,8},{14,10},{16,12},{18,14},{20,16},{2... | collective-permute-start | bytes 98312 | tf_op jit(solution)/shard_map/ppermute | solution.py:15
  210.3 29.8 %collective-permute-start.25 = (f32[32,256]{1,0:T(8,128)}, f32[32,256]{1,0:T(8,128)S(1)}, u32[]{:S(2)}, u32[]{:S(2)}) collective-permute-start(f32[32,256]{1,0:T(8,128)} %reduce-scatter.5.cloned.1.call-done), channel_id=1, source_target_pairs={{22,0},{24,2},{26,4},{28,6},{30,8},{0,10},{2,12},{4,14},{6,16},{8,... | collective-permute-start | bytes 98312 | tf_op jit(solution)/shard_map/ppermute | solution.py:15
  212.8 27.4 %collective-permute-start.24 = (f32[32,256]{1,0:T(8,128)}, f32[32,256]{1,0:T(8,128)S(1)}, u32[]{:S(2)}, u32[]{:S(2)}) collective-permute-start(f32[32,256]{1,0:T(8,128)} %reduce-scatter.5.cloned.1.call-done), channel_id=1, source_target_pairs={{24,0},{26,2},{28,4},{30,6},{0,8},{2,10},{4,12},{6,14},{8,16},{10,... | collective-permute-start | bytes 98312 | tf_op jit(solution)/shard_map/ppermute | solution.py:15
  214.0 6.6 %collective-permute-start.19 = (f32[32,256]{1,0:T(8,128)}, f32[32,256]{1,0:T(8,128)S(1)}, u32[]{:S(2)}, u32[]{:S(2)}) collective-permute-start(f32[32,256]{1,0:T(8,128)} %reduce-scatter.5.cloned.1.call-done), channel_id=1, source_target_pairs={{6,0},{8,2},{10,4},{12,6},{14,8},{16,10},{18,12},{20,14},{22,16},{... | collective-permute-start | bytes 98312 | tf_op jit(solution)/shard_map/ppermute | solution.py:15
  220.6 5.8 %collective-permute-start.20 = (f32[32,256]{1,0:T(8,128)}, f32[32,256]{1,0:T(8,128)S(1)}, u32[]{:S(2)}, u32[]{:S(2)}) collective-permute-start(f32[32,256]{1,0:T(8,128)} %reduce-scatter.5.cloned.1.call-done), channel_id=1, source_target_pairs={{8,0},{10,2},{12,4},{14,6},{16,8},{18,10},{20,12},{22,14},{24,16},... | collective-permute-start | bytes 98312 | tf_op jit(solution)/shard_map/ppermute | solution.py:15
  233.5 6.6 %collective-permute-start.23 = (f32[32,256]{1,0:T(8,128)}, f32[32,256]{1,0:T(8,128)S(1)}, u32[]{:S(2)}, u32[]{:S(2)}) collective-permute-start(f32[32,256]{1,0:T(8,128)} %reduce-scatter.5.cloned.1.call-done), channel_id=1, source_target_pairs={{26,0},{28,2},{30,4},{0,6},{2,8},{4,10},{6,12},{8,14},{10,16},{12,... | collective-permute-start | bytes 98312 | tf_op jit(solution)/shard_map/ppermute | solution.py:15
  (25 other events, 237.1 us)
Sparse Core Ops, SparseCore 0:
  25.7 16.0 reduce-scatter.2
  196.9 12.6 reduce-scatter.4
where the time goes:
time: 318 us; the launch traced here: 316 us
  starting transfers between devices  59.5 us (19%)
  local copies, waits for them, and re-layouts  57 us (18%)
  blocking collectives  51.2 us (16%)
  matrix products  48.7 us (15%)
  loops' own time  41 us (13%)
  waiting for transfers between devices  31.1 us (10%)
  other arithmetic  13.9 us (4%)
  between operations  13.9 us (4%)
    ppermute x26, starting transfers between devices, from_behind(): return lax.ppermute(block, axis, route)  59.5 us
    another operation x2, loops' own time, couple_chips(): return lax.fori_loop(0, used_count, add_slot, start_value)  41 us
    psum x1, blocking collectives, on_device(): lax.psum(jnp.sum(first_pass * first_pass, axis=1), ('leaf', 'sub'))  39.2 us
    ppermute x26, waiting for transfers between devices, from_behind(): return lax.ppermute(block, axis, route)  20.7 us
    dynamic_slice x16, local copies, waits for them, and re-layouts, add_slot(): source = stacked[slot_place[slot_index]]  20.5 us
    dot_general x2, matrix products, apply_matrix(): jnp.einsum('clnp,lnpq->clq', source_values, kernels, precision=highest)  19.5 us
    dot_general x16, matrix products, add_slot(): jnp.dot(source, far_chip_blocks[slot_index], precision=highest, preferred...  19.2 us
    all_gather x2, blocking collectives, chip_level(): coupled = lax.all_gather(coupled_half, 'sub', axis=0, tiled=True)  11.9 us
  transfers between devices with their start and end apart: 28, of which 11 were waited for; matrix products, arithmetic and copies ran while one was open for 22% of the time, Pallas kernels for 0%

commit v1 on v0

--- a/solution.py
+++ b/solution.py
@@ -146,7 +146,7 @@
         far_chip_blocks,
         leaf_total,
     )
-    squares = lax.psum(jnp.sum(first_pass * first_pass, axis=1), ("leaf", "sub"))
+    squares = lax.psum(lax.psum(jnp.sum(first_pass * first_pass, axis=1), "sub"), "leaf")
     column_scale = lax.rsqrt(squares / point_total + epsilon)
     second = apply_matrix(
         first_pass * column_scale[:, None],

time: 318 us -> 317 us (level)
  blocking collectives: 51.2 us -> 39.4 us
  starting transfers between devices: 59.5 us -> 65.8 us
  loops' own time: 41 us -> 44.2 us
    psum x1 -> x2, blocking collectives: 39.2 us -> 27.4 us  [the longest x1 25 us: on_device(): lax.psum(lax.psum(jnp.sum(first_pass * first_pass, axis=1), 'sub'), 'leaf')]
    ppermute x26, starting transfers between devices: 59.5 us -> 65.8 us  [from_behind(): return lax.ppermute(block, axis, route)]
where the time goes in v1:
time: 317 us; the launch traced here: 315 us
  starting transfers between devices  65.8 us (21%)
  local copies, waits for them, and re-layouts  56.2 us (18%)
  matrix products  48.7 us (15%)
  loops' own time  44.2 us (14%)
  blocking collectives  39.4 us (12%)
  waiting for transfers between devices  32.8 us (10%)
  between operations  13.9 us (4%)
  other arithmetic  13.7 us (4%)
    ppermute x26, starting transfers between devices, from_behind(): return lax.ppermute(block, axis, route)  65.8 us
    another operation x2, loops' own time, couple_chips(): return lax.fori_loop(0, used_count, add_slot, start_value)  44.2 us
    psum x1, blocking collectives, on_device(): lax.psum(lax.psum(jnp.sum(first_pass * first_pass, axis=1), 'sub'), 'leaf')  25 us
    ppermute x26, waiting for transfers between devices, from_behind(): return lax.ppermute(block, axis, route)  20.6 us
    dynamic_slice x16, local copies, waits for them, and re-layouts, add_slot(): source = stacked[slot_place[slot_index]]  19.7 us
    dot_general x2, matrix products, apply_matrix(): jnp.einsum('clnp,lnpq->clq', source_values, kernels, precision=highest)  19.5 us
    dot_general x16, matrix products, add_slot(): jnp.dot(source, far_chip_blocks[slot_index], precision=highest, preferred...  19.2 us
    reduce_scatter x2, waiting for transfers between devices, chip_level(): halves = lax.psum_scatter(upward, 'sub', scatter_dimension=0, tiled=True)  12.2 us
  transfers between devices with their start and end apart: 28, of which 11 were waited for; matrix products, arithmetic and copies ran while one was open for 22% of the time, Pallas kernels for 0%

profile of v1, /device:TPU:5, one launch (start us, length us, event | category | flops | bytes accessed | tf_op | source)
XLA Modules:
  0.0 314.7 jit_solution(10121775175738408827)
XLA Ops:
  9.1 4.0 %gather_fusion.2 = f32[1024,64]{1,0:T(8,128)} fusion(f32[64,1024]{0,1:T(8,128)S(1)} %copy.43, s32[1024]{0:T(1024)S(1)} %get-tuple-element.107), kind=kCustom, calls=%fused_computation.6 | custom fusion | bytes 528384 | tf_op jit(solution)/shard_map/gather | solution.py:129
  18.9 3.8 %gather_fusion = f32[1024,3]{1,0:T(8,128)S(1)} fusion(f32[3,1024]{0,1:T(8,128)} %copy.39, s32[1024]{0:T(1024)S(1)} %get-tuple-element.107), kind=kCustom, calls=%fused_computation.4 | custom fusion | bytes 28672 | tf_op jit(solution)/shard_map/gather | solution.py:130
  45.1 5.9 %collective-permute-start.6 = (f32[32,256]{1,0:T(8,128)}, f32[32,256]{1,0:T(8,128)S(1)}, u32[]{:S(2)}, u32[]{:S(2)}) collective-permute-start(f32[32,256]{1,0:T(8,128)} %reduce-scatter.3.cloned.1.call-done), channel_id=1, source_target_pairs={{4,0},{6,2},{8,4},{10,6},{12,8},{14,10},{16,12},{18,14},{20,16},{2... | collective-permute-start | bytes 98312 | tf_op jit(solution)/shard_map/ppermute | solution.py:15
  54.8 10.9 %collective-permute-start.7 = (f32[32,256]{1,0:T(8,128)}, f32[32,256]{1,0:T(8,128)S(1)}, u32[]{:S(2)}, u32[]{:S(2)}) collective-permute-start(f32[32,256]{1,0:T(8,128)} %reduce-scatter.3.cloned.1.call-done), channel_id=1, source_target_pairs={{6,0},{8,2},{10,4},{12,6},{14,8},{16,10},{18,12},{20,14},{22,16},{... | collective-permute-start | bytes 98312 | tf_op jit(solution)/shard_map/ppermute | solution.py:15
  67.3 3.2 %collective-permute-done.8 = f32[32,256]{1,0:T(8,128)S(1)} collective-permute-done((f32[32,256]{1,0:T(8,128)}, f32[32,256]{1,0:T(8,128)S(1)}, u32[]{:S(2)}, u32[]{:S(2)}) %collective-permute-start.8) | collective-permute-done | bytes 32800 | tf_op jit(solution)/shard_map/ppermute | solution.py:15
  70.5 5.1 %collective-permute-start.9 = (f32[32,256]{1,0:T(8,128)}, f32[32,256]{1,0:T(8,128)S(1)}, u32[]{:S(2)}, u32[]{:S(2)}) collective-permute-start(f32[32,256]{1,0:T(8,128)} %reduce-scatter.3.cloned.1.call-done), channel_id=1, source_target_pairs={{10,0},{12,2},{14,4},{16,6},{18,8},{20,10},{22,12},{24,14},{26,16}... | collective-permute-start | bytes 98312 | tf_op jit(solution)/shard_map/ppermute | solution.py:15
  82.7 3.7 %collective-permute-done.11 = f32[32,256]{1,0:T(8,128)S(1)} collective-permute-done((f32[32,256]{1,0:T(8,128)}, f32[32,256]{1,0:T(8,128)S(1)}, u32[]{:S(2)}, u32[]{:S(2)}) %collective-permute-start.11) | collective-permute-done | bytes 32800 | tf_op jit(solution)/shard_map/ppermute | solution.py:15
  87.1 41.1 %while.20 = (s32[]{:T(128)}, f32[32,256]{1,0:T(8,128)S(1)}, s32[]{:T(128)}, s32[8]{0:T(128)}, f32[8,32,256]{2,1,0:T(8,128)}, /*index=5*/f32[8,256,256]{2,1,0:T(8,128)}, s32[]{:T(128)}, s32[]{:T(128)}, s32[]{:T(128)}) while((s32[]{:T(128)}, f32[32,256]{1,0:T(8,128)S(1)}, s32[]{:T(128)}, s32[8]{0:T(128)}, f32[8,32,256]{2,1,0:T(8,128)}, ...), condition=%wide.region_3.6_spmd, body=%wide.region_2.5_spmd.sunk | while | flops 25174024 | bytes 360637 | solution.py:50
  128.3 3.8 %all_gather.6 = f32[64,256]{1,0:T(8,128)S(1)} all-gather(f32[32,256]{1,0:T(8,128)S(1)} %get-tuple-element.73), channel_id=1, replica_groups=mesh['leaf'=16,'sub'=2] {'sub'}, dimensions={0}, use_global_device_ids=true | all-gather | bytes 98304 | tf_op jit(solution)/shard_map/all_gather | solution.py:69
  135.2 3.6 %gather_fusion.3 = f32[8,64,512]{1,2,0:T(8,128)} fusion(f32[64,6,512]{0,2,1:T(8,128)} %bitcast.168, s32[1024]{0:T(1024)} %pad_clamp_fusion.1), kind=kCustom, calls=%fused_computation.clone | custom fusion | bytes 2097184 | tf_op jit(solution)/shard_map/jit(_take)/gather | solution.py:89
  138.8 3.2 %copy.44 = f32[8,64,512]{2,1,0:T(8,128)} copy(f32[8,64,512]{1,2,0:T(8,128)} %gather_fusion.3) | data formatting | bytes 2097152 | tf_op jit(solution)/shard_map/jit(_take)/gather | solution.py:89
  142.0 9.7 %fusion.26 = f32[64,2,512]{2,0,1:T(8,128)S(1)} fusion(f32[2,512]{1,0:T(2,128)S(1)} %copy-done.13, f32[2,4,512]{2,1,0:T(4,128)S(1)} %copy-done.5, f32[2,512]{1,0:T(2,128)S(1)} %copy-done.11, f32[2,4,512]{2,1,0:T(4,128)S(1)} %copy-done.7, f32[2,512]{1,0:T(2,128)S(1)} %copy-done.9, f32[2,4,512]{2,1,0:T(4,128)S(1)} %bitcast.184, ...), kind=kOutput, calls=%fused_computation.38 | convolution fusion | flops 1629749248 | bytes 1372168 | tf_op jit(solution)/shard_map/clnp,lnpq->clq/dot_general | solution.py:90
  153.0 2.5 psum.14
  155.4 25.0 %psum.15 = f32[64]{0:T(128)S(1)} all-reduce(f32[64]{0:T(128)S(1)} %psum.14), channel_id=1, replica_groups=mesh['leaf'=16,'sub'=2] {'leaf'}, use_global_device_ids=true, to_apply=%region_6.9 | all-reduce | flops 64 | bytes 512 | tf_op jit(solution)/shard_map/psum | solution.py:149
  181.2 7.2 %collective-permute-start.17 = (f32[2,64,256]{2,1,0:T(8,128)S(1)}, f32[2,64,256]{2,1,0:T(8,128)S(1)}, u32[]{:S(2)}, u32[]{:S(2)}) collective-permute-start(f32[2,64,256]{2,1,0:T(8,128)S(1)} %fusion.41), channel_id=1, source_target_pairs={{1,0},{2,1},{3,2},{4,3},{5,4},{6,5},{7,6},{8,7},{9,8},{10,9},{11,1... | collective-permute-start | bytes 393224 | tf_op jit(solution)/shard_map/ppermute | solution.py:15
  196.0 12.2 %reduce-scatter.5.cloned.1.call-done = f32[32,256]{1,0:T(8,128)} async-done(((f32[64,256]{1,0:T(8,128)}), f32[32,256]{1,0:T(8,128)}) %reduce-scatter.5.cloned.1.call-update) | async-done | bytes 32784 | tf_op jit(solution)/shard_map/reduce_scatter | solution.py:66
  212.6 5.2 %collective-permute-start.19 = (f32[32,256]{1,0:T(8,128)}, f32[32,256]{1,0:T(8,128)S(1)}, u32[]{:S(2)}, u32[]{:S(2)}) collective-permute-start(f32[32,256]{1,0:T(8,128)} %reduce-scatter.5.cloned.1.call-done), channel_id=1, source_target_pairs={{6,0},{8,2},{10,4},{12,6},{14,8},{16,10},{18,12},{20,14},{22,16},{... | collective-permute-start | bytes 98312 | tf_op jit(solution)/shard_map/ppermute | solution.py:15
  219.2 4.5 %collective-permute-start.20 = (f32[32,256]{1,0:T(8,128)}, f32[32,256]{1,0:T(8,128)S(1)}, u32[]{:S(2)}, u32[]{:S(2)}) collective-permute-start(f32[32,256]{1,0:T(8,128)} %reduce-scatter.5.cloned.1.call-done), channel_id=1, source_target_pairs={{8,0},{10,2},{12,4},{14,6},{16,8},{18,10},{20,12},{22,14},{24,16},... | collective-permute-start | bytes 98312 | tf_op jit(solution)/shard_map/ppermute | solution.py:15
  225.0 2.6 collective-permute-start.21
  234.6 4.2 %collective-permute-done.23 = f32[32,256]{1,0:T(8,128)S(1)} collective-permute-done((f32[32,256]{1,0:T(8,128)}, f32[32,256]{1,0:T(8,128)S(1)}, u32[]{:S(2)}, u32[]{:S(2)}) %collective-permute-start.23) | collective-permute-done | bytes 32800 | tf_op jit(solution)/shard_map/ppermute | solution.py:15
  238.8 42.0 %while.21 = (s32[]{:T(128)}, f32[32,256]{1,0:T(8,128)S(1)}, s32[]{:T(128)}, s32[8]{0:T(128)}, f32[8,32,256]{2,1,0:T(8,128)S(1)}, /*index=5*/f32[8,256,256]{2,1,0:T(8,128)}, s32[]{:T(128)}, s32[]{:T(128)}, s32[]{:T(128)}) while((s32[]{:T(128)}, f32[32,256]{1,0:T(8,128)S(1)}, s32[]{:T(128)}, s32[8]{0:T(128)}, f32[8,32,256]{2,1,0:T(8,128)S(1)}, ...), condition=%wide.region_9.12_spmd, body=%wide.region_8.11_spmd.sunk | while | flops 25174024 | bytes 360637 | solution.py:50
  280.8 8.1 %all_gather.7 = f32[64,256]{1,0:T(8,128)S(1)} all-gather(f32[32,256]{1,0:T(8,128)S(1)} %get-tuple-element.74), channel_id=1, replica_groups=mesh['leaf'=16,'sub'=2] {'sub'}, dimensions={0}, use_global_device_ids=true | all-gather | bytes 98304 | tf_op jit(solution)/shard_map/all_gather | solution.py:69
  292.6 9.7 %fusion.27 = f32[64,2,512]{2,0,1:T(8,128)S(1)} fusion(f32[2,512]{1,0:T(2,128)S(1)} %copy-done.14, f32[2,4,512]{2,1,0:T(4,128)S(1)} %copy-done.6, f32[2,512]{1,0:T(2,128)S(1)} %copy-done.12, f32[2,4,512]{2,1,0:T(4,128)S(1)} %copy-done.8, f32[2,512]{1,0:T(2,128)S(1)} %copy-done.10, f32[2,4,512]{2,1,0:T(4,128)S(1)} %bitcast.185, ...), kind=kOutput, calls=%fused_computation.39 | convolution fusion | flops 1629749248 | bytes 1372168 | tf_op jit(solution)/shard_map/clnp,lnpq->clq/dot_general | solution.py:90
  303.7 3.3 %scatter_custom_fusion = f32[64,1024]{0,1:T(8,128)S(1)} fusion(s32[1024]{0:T(1024)} %get-tuple-element.108, f32[1024,64]{1,0:T(8,128)S(1)} %copy.49, f32[]{:T(128)} %constant.109.clone.1), kind=kCustom, calls=%fused_computation.71 | custom fusion | bytes 262656 | tf_op jit(solution)/shard_map/scatter | solution.py:163
  (191 shorter events, 115.2 us)
Async XLA Ops:
  6.5 38.6 %reduce-scatter.3.cloned.1.call-start = ((), (), s32[]{:S(2)}) async-start(), calls=%async_computation.2 | async-start | bytes 98304 | tf_op jit(solution)/shard_map/reduce_scatter | solution.py:66
  15.3 28.4 %collective-permute-start.5 = (f32[2,64,256]{2,1,0:T(8,128)S(1)}, f32[2,64,256]{2,1,0:T(8,128)S(1)}, u32[]{:S(2)}, u32[]{:S(2)}) collective-permute-start(f32[2,64,256]{2,1,0:T(8,128)S(1)} %fusion.58), channel_id=1, source_target_pairs={{1,0},{2,1},{3,2},{4,3},{5,4},{6,5},{7,6},{8,7},{9,8},{10,9},{11,1... | collective-permute-start | bytes 393224 | tf_op jit(solution)/shard_map/ppermute | solution.py:15
  16.0 27.7 %collective-permute-start.4 = (f32[2,64,256]{2,1,0:T(8,128)S(1)}, f32[2,64,256]{2,1,0:T(8,128)S(1)}, u32[]{:S(2)}, u32[]{:S(2)}) collective-permute-start(f32[2,64,256]{2,1,0:T(8,128)S(1)} %fusion.58), channel_id=1, source_target_pairs={{31,0},{0,1},{1,2},{2,3},{3,4},{4,5},{5,6},{6,7},{7,8},{8,9},{9,10... | collective-permute-start | bytes 393224 | tf_op jit(solution)/shard_map/ppermute | solution.py:15
  22.8 13.8 %collective-permute-start.1 = (f32[3,1024]{0,1:T(8,128)S(1)}, f32[3,1024]{0,1:T(8,128)}, u32[]{:S(2)}, u32[]{:S(2)}) collective-permute-start(f32[3,1024]{0,1:T(8,128)S(1)} %bitcast.164), channel_id=1, source_target_pairs={{1,0},{2,1},{3,2},{4,3},{5,4},{6,5},{7,6},{8,7},{9,8},{10,9},{11,1... | collective-permute-start | bytes 36872 | tf_op jit(solution)/shard_map/ppermute | solution.py:15
  22.8 16.7 %collective-permute-start = (f32[3,1024]{0,1:T(8,128)S(1)}, f32[3,1024]{0,1:T(8,128)}, u32[]{:S(2)}, u32[]{:S(2)}) collective-permute-start(f32[3,1024]{0,1:T(8,128)S(1)} %bitcast.165), channel_id=1, source_target_pairs={{31,0},{0,1},{1,2},{2,3},{3,4},{4,5},{5,6},{6,7},{7,8},{8,9},{9,10... | collective-permute-start | bytes 36872 | tf_op jit(solution)/shard_map/ppermute | solution.py:15
  25.6 182.6 %reduce-scatter.5.cloned.1.call-start = ((), (), s32[]{:S(2)}) async-start(), calls=%async_computation.3 | async-start | bytes 98304 | tf_op jit(solution)/shard_map/reduce_scatter | solution.py:66
  25.7 107.0 %collective-permute-start.3 = (f32[64,1024]{0,1:T(8,128)}, f32[64,1024]{0,1:T(8,128)}, u32[]{:S(2)}, u32[]{:S(2)}) collective-permute-start(f32[64,1024]{0,1:T(8,128)} %bitcast.171), channel_id=1, source_target_pairs={{1,0},{2,1},{3,2},{4,3},{5,4},{6,5},{7,6},{8,7},{9,8},{10,9},{11,1... | collective-permute-start | bytes 786440 | tf_op jit(solution)/shard_map/ppermute | solution.py:15
  36.6 96.1 %collective-permute-start.2 = (f32[64,1024]{0,1:T(8,128)}, f32[64,1024]{0,1:T(8,128)}, u32[]{:S(2)}, u32[]{:S(2)}) collective-permute-start(f32[64,1024]{0,1:T(8,128)} %bitcast.172), channel_id=1, source_target_pairs={{31,0},{0,1},{1,2},{2,3},{3,4},{4,5},{5,6},{6,7},{7,8},{8,9},{9,10... | collective-permute-start | bytes 786440 | tf_op jit(solution)/shard_map/ppermute | solution.py:15
  45.1 9.7 %collective-permute-start.6 = (f32[32,256]{1,0:T(8,128)}, f32[32,256]{1,0:T(8,128)S(1)}, u32[]{:S(2)}, u32[]{:S(2)}) collective-permute-start(f32[32,256]{1,0:T(8,128)} %reduce-scatter.3.cloned.1.call-done), channel_id=1, source_target_pairs={{4,0},{6,2},{8,4},{10,6},{12,8},{14,10},{16,12},{18,14},{20,16},{2... | collective-permute-start | bytes 98312 | tf_op jit(solution)/shard_map/ppermute | solution.py:15
  51.8 34.6 %collective-permute-start.13 = (f32[32,256]{1,0:T(8,128)}, f32[32,256]{1,0:T(8,128)S(1)}, u32[]{:S(2)}, u32[]{:S(2)}) collective-permute-start(f32[32,256]{1,0:T(8,128)} %reduce-scatter.3.cloned.1.call-done), channel_id=1, source_target_pairs={{22,0},{24,2},{26,4},{28,6},{30,8},{0,10},{2,12},{4,14},{6,16},{8,... | collective-permute-start | bytes 98312 | tf_op jit(solution)/shard_map/ppermute | solution.py:15
  53.5 32.9 %collective-permute-start.12 = (f32[32,256]{1,0:T(8,128)}, f32[32,256]{1,0:T(8,128)S(1)}, u32[]{:S(2)}, u32[]{:S(2)}) collective-permute-start(f32[32,256]{1,0:T(8,128)} %reduce-scatter.3.cloned.1.call-done), channel_id=1, source_target_pairs={{24,0},{26,2},{28,4},{30,6},{0,8},{2,10},{4,12},{6,14},{8,16},{10,... | collective-permute-start | bytes 98312 | tf_op jit(solution)/shard_map/ppermute | solution.py:15
  54.8 12.3 %collective-permute-start.7 = (f32[32,256]{1,0:T(8,128)}, f32[32,256]{1,0:T(8,128)S(1)}, u32[]{:S(2)}, u32[]{:S(2)}) collective-permute-start(f32[32,256]{1,0:T(8,128)} %reduce-scatter.3.cloned.1.call-done), channel_id=1, source_target_pairs={{6,0},{8,2},{10,4},{12,6},{14,8},{16,10},{18,12},{20,14},{22,16},{... | collective-permute-start | bytes 98312 | tf_op jit(solution)/shard_map/ppermute | solution.py:15
  70.5 6.4 %collective-permute-start.9 = (f32[32,256]{1,0:T(8,128)}, f32[32,256]{1,0:T(8,128)S(1)}, u32[]{:S(2)}, u32[]{:S(2)}) collective-permute-start(f32[32,256]{1,0:T(8,128)} %reduce-scatter.3.cloned.1.call-done), channel_id=1, source_target_pairs={{10,0},{12,2},{14,4},{16,6},{18,8},{20,10},{22,12},{24,14},{26,16}... | collective-permute-start | bytes 98312 | tf_op jit(solution)/shard_map/ppermute | solution.py:15
  80.3 6.1 %collective-permute-start.11 = (f32[32,256]{1,0:T(8,128)}, f32[32,256]{1,0:T(8,128)S(1)}, u32[]{:S(2)}, u32[]{:S(2)}) collective-permute-start(f32[32,256]{1,0:T(8,128)} %reduce-scatter.3.cloned.1.call-done), channel_id=1, source_target_pairs={{26,0},{28,2},{30,4},{0,6},{2,8},{4,10},{6,12},{8,14},{10,16},{12,... | collective-permute-start | bytes 98312 | tf_op jit(solution)/shard_map/ppermute | solution.py:15
  181.2 12.5 %collective-permute-start.17 = (f32[2,64,256]{2,1,0:T(8,128)S(1)}, f32[2,64,256]{2,1,0:T(8,128)S(1)}, u32[]{:S(2)}, u32[]{:S(2)}) collective-permute-start(f32[2,64,256]{2,1,0:T(8,128)S(1)} %fusion.41), channel_id=1, source_target_pairs={{1,0},{2,1},{3,2},{4,3},{5,4},{6,5},{7,6},{8,7},{9,8},{10,9},{11,1... | collective-permute-start | bytes 393224 | tf_op jit(solution)/shard_map/ppermute | solution.py:15
  188.4 5.3 %collective-permute-start.16 = (f32[2,64,256]{2,1,0:T(8,128)S(1)}, f32[2,64,256]{2,1,0:T(8,128)}, u32[]{:S(2)}, u32[]{:S(2)}) collective-permute-start(f32[2,64,256]{2,1,0:T(8,128)S(1)} %fusion.41), channel_id=1, source_target_pairs={{31,0},{0,1},{1,2},{2,3},{3,4},{4,5},{5,6},{6,7},{7,8},{8,9},{9,10... | collective-permute-start | bytes 393224 | tf_op jit(solution)/shard_map/ppermute | solution.py:15
  190.9 98.6 %collective-permute-start.15 = (f32[64,1024]{1,0:T(8,128)}, f32[64,1024]{1,0:T(8,128)}, u32[]{:S(2)}, u32[]{:S(2)}) collective-permute-start(f32[64,1024]{1,0:T(8,128)} %broadcast_multiply_fusion), channel_id=1, source_target_pairs={{1,0},{2,1},{3,2},{4,3},{5,4},{6,5},{7,6},{8,7},{9,8},{10,9},{11,1... | collective-permute-start | bytes 786440 | tf_op jit(solution)/shard_map/ppermute | solution.py:15
  190.9 98.6 %collective-permute-start.14 = (f32[64,1024]{1,0:T(8,128)}, f32[64,1024]{1,0:T(8,128)}, u32[]{:S(2)}, u32[]{:S(2)}) collective-permute-start(f32[64,1024]{1,0:T(8,128)} %broadcast_multiply_fusion), channel_id=1, source_target_pairs={{31,0},{0,1},{1,2},{2,3},{3,4},{4,5},{5,6},{6,7},{7,8},{8,9},{9,10... | collective-permute-start | bytes 786440 | tf_op jit(solution)/shard_map/ppermute | solution.py:15
  208.2 4.4 %collective-permute-start.18 = (f32[32,256]{1,0:T(8,128)}, f32[32,256]{1,0:T(8,128)S(1)}, u32[]{:S(2)}, u32[]{:S(2)}) collective-permute-start(f32[32,256]{1,0:T(8,128)} %reduce-scatter.5.cloned.1.call-done), channel_id=1, source_target_pairs={{4,0},{6,2},{8,4},{10,6},{12,8},{14,10},{16,12},{18,14},{20,16},{2... | collective-permute-start | bytes 98312 | tf_op jit(solution)/shard_map/ppermute | solution.py:15
  208.9 29.8 %collective-permute-start.25 = (f32[32,256]{1,0:T(8,128)}, f32[32,256]{1,0:T(8,128)S(1)}, u32[]{:S(2)}, u32[]{:S(2)}) collective-permute-start(f32[32,256]{1,0:T(8,128)} %reduce-scatter.5.cloned.1.call-done), channel_id=1, source_target_pairs={{22,0},{24,2},{26,4},{28,6},{30,8},{0,10},{2,12},{4,14},{6,16},{8,... | collective-permute-start | bytes 98312 | tf_op jit(solution)/shard_map/ppermute | solution.py:15
  211.4 27.4 %collective-permute-start.24 = (f32[32,256]{1,0:T(8,128)}, f32[32,256]{1,0:T(8,128)S(1)}, u32[]{:S(2)}, u32[]{:S(2)}) collective-permute-start(f32[32,256]{1,0:T(8,128)} %reduce-scatter.5.cloned.1.call-done), channel_id=1, source_target_pairs={{24,0},{26,2},{28,4},{30,6},{0,8},{2,10},{4,12},{6,14},{8,16},{10,... | collective-permute-start | bytes 98312 | tf_op jit(solution)/shard_map/ppermute | solution.py:15
  212.6 6.6 %collective-permute-start.19 = (f32[32,256]{1,0:T(8,128)}, f32[32,256]{1,0:T(8,128)S(1)}, u32[]{:S(2)}, u32[]{:S(2)}) collective-permute-start(f32[32,256]{1,0:T(8,128)} %reduce-scatter.5.cloned.1.call-done), channel_id=1, source_target_pairs={{6,0},{8,2},{10,4},{12,6},{14,8},{16,10},{18,12},{20,14},{22,16},{... | collective-permute-start | bytes 98312 | tf_op jit(solution)/shard_map/ppermute | solution.py:15
  219.2 5.8 %collective-permute-start.20 = (f32[32,256]{1,0:T(8,128)}, f32[32,256]{1,0:T(8,128)S(1)}, u32[]{:S(2)}, u32[]{:S(2)}) collective-permute-start(f32[32,256]{1,0:T(8,128)} %reduce-scatter.5.cloned.1.call-done), channel_id=1, source_target_pairs={{8,0},{10,2},{12,4},{14,6},{16,8},{18,10},{20,12},{22,14},{24,16},... | collective-permute-start | bytes 98312 | tf_op jit(solution)/shard_map/ppermute | solution.py:15
  232.1 6.6 %collective-permute-start.23 = (f32[32,256]{1,0:T(8,128)}, f32[32,256]{1,0:T(8,128)S(1)}, u32[]{:S(2)}, u32[]{:S(2)}) collective-permute-start(f32[32,256]{1,0:T(8,128)} %reduce-scatter.5.cloned.1.call-done), channel_id=1, source_target_pairs={{26,0},{28,2},{30,4},{0,6},{2,8},{4,10},{6,12},{8,14},{10,16},{12,... | collective-permute-start | bytes 98312 | tf_op jit(solution)/shard_map/ppermute | solution.py:15
  (25 other events, 239.2 us)
Sparse Core Ops, SparseCore 0:
  25.7 16.0 reduce-scatter.2
  193.8 14.3 reduce-scatter.4
